TPU v7x, 128 devices: a whole 4x4x4 slice. The times are simulated.
128 devices in a mesh: seq: 4 (over y_lo, core), tensor: 32 (over z, x, y_hi).
Axes of the slice: x: 4, y: 4 (y_hi: 2, y_lo: 2; y = y_hi * 2 + y_lo), z: 4, core: 2. Of those that a mesh axis runs over, the one named last changes fastest.
Arguments:
- tokens: bfloat16 [1024, 8192], P(('seq', 'tensor')), may hold values from -6 to 6
- gate_blocks: bfloat16 [32, 336, 128, 128], P('tensor', 'seq'), may hold values from -0.09375 to 0.09375
- gate_slots: int32 [32, 336], P('tensor', 'seq'), may hold values from 0 to 447, as said below
- up_blocks: bfloat16 [32, 336, 128, 128], P('tensor', 'seq'), may hold values from -0.09375 to 0.09375
- up_slots: int32 [32, 336], P('tensor', 'seq'), may hold values from 0 to 447, as said below
- down_blocks: bfloat16 [32, 336, 128, 128], P('tensor', 'seq'), may hold values from -0.046875 to 0.046875
- down_slots: int32 [32, 336], P('tensor', 'seq'), may hold values from 0 to 447, as said below
- block_counts: int32 [32, 3], P('tensor'), may hold values from 84 to 336, as said below
Outputs:
- layer_out: bfloat16 [1024, 8192], P(('seq', 'tensor'))
Inputs may be any that keep to these rules, and one draw needn't show every extreme that they name: `gate_slots`: within each shard the 336 entries are distinct; only the first block_counts[s, 0] entries of shard s are used. `up_slots`: within each shard the 336 entries are distinct; only the first block_counts[s, 1] entries of shard s are used. `down_slots`: within each shard the 336 entries are distinct; only the first block_counts[s, 2] entries of shard s are used. `block_counts`: for each of the three matrices some shard has exactly 336 live slots in every draw.
All inputs are finite; a program needn't handle non-finite values.
Results may differ from a plain program's by a relative error of at most 0.0049.
Values may be sent and summed in bfloat16 or wider, within the bound.
A program may use at most 192 MiB of HBM per device.

v0:
```python
import jax
import jax.numpy as jnp
from jax import lax
from jax.sharding import PartitionSpec as P

FF = 28672


def place_blocks(values, slot_ids, live_mask, stacked):
    block_size = values.shape[-1]
    one_hot = jnp.where(
        live_mask[:, None] & (slot_ids[:, None] == jnp.arange(stacked, dtype=jnp.int32)[None, :]),
        1.0,
        0.0,
    ).astype(jnp.bfloat16)
    flattened = values.reshape(values.shape[0], block_size * block_size)
    placed = lax.dot_general(
        one_hot, flattened, (((0,), (0,)), ((), ())), preferred_element_type=jnp.float32
    )
    return placed.astype(jnp.bfloat16)


def arrange_blocks(placed, outer_count, inner_count, block_size):
    shaped = placed.reshape(outer_count, inner_count, block_size, block_size)
    return shaped.transpose(0, 2, 1, 3).reshape(outer_count * block_size, inner_count * block_size)


def on_device(
    tokens, gate_blocks, gate_slots, up_blocks, up_slots, down_blocks, down_slots, block_counts
):
    block_size = gate_blocks.shape[-1]
    width = tokens.shape[1]
    row_blocks = width // block_size
    tensor_count = lax.axis_size("tensor")
    shard_blocks = FF // block_size // tensor_count
    stacked = row_blocks * shard_blocks
    gate_values = gate_blocks[0]
    gate_ids = gate_slots[0]
    up_values = up_blocks[0]
    up_ids = up_slots[0]
    down_values = down_blocks[0]
    down_ids = down_slots[0]
    counts = block_counts[0]
    span_rows = lax.all_gather(tokens, "tensor", axis=0, tiled=True)
    part_gate = lax.all_gather(gate_values, "seq", axis=0, tiled=True)
    part_gate_ids = lax.all_gather(gate_ids, "seq", axis=0, tiled=True)
    part_up = lax.all_gather(up_values, "seq", axis=0, tiled=True)
    part_up_ids = lax.all_gather(up_ids, "seq", axis=0, tiled=True)
    positions = jnp.arange(part_gate.shape[0], dtype=jnp.int32)
    gate_front = place_blocks(part_gate, part_gate_ids, positions < counts[0], stacked)
    up_front = place_blocks(part_up, part_up_ids, positions < counts[1], stacked)
    gate_sum = jnp.dot(
        span_rows,
        arrange_blocks(gate_front, row_blocks, shard_blocks, block_size),
        preferred_element_type=jnp.float32,
    )
    up_sum = jnp.dot(
        span_rows,
        arrange_blocks(up_front, row_blocks, shard_blocks, block_size),
        preferred_element_type=jnp.float32,
    )
    hidden = (jax.nn.silu(gate_sum) * up_sum).astype(jnp.bfloat16)
    part_down = lax.all_gather(down_values, "seq", axis=0, tiled=True)
    part_down_ids = lax.all_gather(down_ids, "seq", axis=0, tiled=True)
    positions = jnp.arange(part_down.shape[0], dtype=jnp.int32)
    down_back = place_blocks(part_down, part_down_ids, positions < counts[2], stacked)
    partial_value = jnp.dot(
        hidden,
        arrange_blocks(down_back, shard_blocks, row_blocks, block_size),
        preferred_element_type=jnp.float32,
    )
    layer_out = lax.psum_scatter(partial_value, "tensor", scatter_dimension=0, tiled=True).astype(
        jnp.bfloat16
    )
    return layer_out


def solution(mesh):
    return jax.shard_map(
        on_device,
        mesh=mesh,
        in_specs=(
            P(("seq", "tensor"), None),
            P("tensor", "seq", None, None),
            P("tensor", "seq"),
            P("tensor", "seq", None, None),
            P("tensor", "seq"),
            P("tensor", "seq", None, None),
            P("tensor", "seq"),
            P("tensor", None),
        ),
        out_specs=P(("seq", "tensor"), None),
        check_vma=False,
    )
```

profile of v0, /device:TPU:0, one launch (start us, length us, event | category | flops | bytes accessed | tf_op | source)
XLA Modules:
  0.0 677.5 jit_solution(17686191480460950917)
XLA Ops:
  6.5 0.0 all-gather.13.cloned.1.call-start
  6.5 0.7 all-gather.13.cloned.1.call-update
  7.3 0.0 all-gather.15.cloned.1.call-start
  7.3 0.7 all-gather.15.cloned.1.call-update
  8.0 0.0 all-gather.17.cloned.1.call-start
  8.1 0.7 all-gather.17.cloned.1.call-update
  8.7 0.0 all-gather.11.cloned.1.call-start
  8.8 0.5 all-gather.11.cloned.1.call-update
  9.3 0.0 reduce-scatter.2.cloned.1.call-start
  9.4 1.2 dynamic-slice
  11.3 0.8 bitcast_dynamic-update-slice_fusion
  12.0 0.7 bitcast_dynamic-update-slice_fusion.1
  12.8 0.7 bitcast_dynamic-update-slice_fusion.2
  13.5 5.1 all-reduce.3
  18.6 1.4 fusion.57
  20.1 0.6 iota_compare_fusion.5
  20.7 0.7 iota_compare_fusion.4
  21.4 0.7 iota_compare_fusion.3
  22.1 91.0 %all-gather.13.cloned.1.call-done = bf16[1,336,128,128]{3,2,0,1:T(8,128)(2,1)} async-done(((bf16[1,84,128,128]{3,2,0,1:T(8,128)(2,1)}), bf16[1,336,128,128]{3,2,0,1:T(8,128)(2,1)}) %all-gather.13.cloned.1.call-update) | async-done | bytes 11010064 | tf_op jit(solution)/shard_map/all_gather | solution.py:45
  113.1 18.6 %fusion.15 = bf16[56,8,128,128]{3,1,2,0:T(8,128)(2,1)} fusion(bf16[42,8,128,128]{3,2,1,0:T(8,128)(2,1)} %bitcast.110, s32[336]{0:T(512)S(1)} %get-tuple-element.6, pred[336]{0:T(512)(128)(4,1)S(1)} %iota_compare_fusion.5), kind=kOutput, calls=%fused_computation.18 | convolution fusion | flops 4940443648 | bytes 25691792 | tf_op jit(solution)/shard_map/dot_general | solution.py:17
  131.7 14.9 %copy.19 = bf16[56,8,128,128]{3,2,1,0:T(8,128)(2,1)} copy(bf16[56,8,128,128]{3,1,2,0:T(8,128)(2,1)} %fusion.15) | data formatting | bytes 29360128
  146.5 20.3 %copy.13 = bf16[64,7,128,128]{2,0,3,1:T(8,128)(2,1)} copy(bf16[64,7,128,128]{3,2,1,0:T(8,128)(2,1)} %bitcast.102) | data formatting | bytes 29360128 | tf_op jit(solution)/shard_map/reshape | solution.py:24
  166.8 52.0 %all-gather.15.cloned.1.call-done = bf16[1,336,128,128]{3,2,0,1:T(8,128)(2,1)} async-done(((bf16[1,84,128,128]{3,2,0,1:T(8,128)(2,1)}), bf16[1,336,128,128]{3,2,0,1:T(8,128)(2,1)}) %all-gather.15.cloned.1.call-update) | async-done | bytes 11010064 | tf_op jit(solution)/shard_map/all_gather | solution.py:47
  218.8 19.1 %fusion.18 = bf16[56,8,128,128]{3,1,2,0:T(8,128)(2,1)} fusion(bf16[42,8,128,128]{3,2,1,0:T(8,128)(2,1)} %bitcast.109, s32[336]{0:T(512)S(1)} %get-tuple-element.5, pred[336]{0:T(512)(128)(4,1)S(1)} %iota_compare_fusion.4), kind=kOutput, calls=%fused_computation.19 | convolution fusion | flops 4940443648 | bytes 25691792 | tf_op jit(solution)/shard_map/dot_general | solution.py:17
  238.0 14.7 %copy.22 = bf16[56,8,128,128]{3,2,1,0:T(8,128)(2,1)} copy(bf16[56,8,128,128]{3,1,2,0:T(8,128)(2,1)} %fusion.18) | data formatting | bytes 29360128
  252.7 20.3 %copy.15 = bf16[64,7,128,128]{2,0,3,1:T(8,128)(2,1)} copy(bf16[64,7,128,128]{3,2,1,0:T(8,128)(2,1)} %bitcast.103) | data formatting | bytes 29360128 | tf_op jit(solution)/shard_map/reshape | solution.py:24
  273.0 51.6 %all-gather.17.cloned.1.call-done = bf16[1,336,128,128]{3,2,0,1:T(8,128)(2,1)} async-done(((bf16[1,84,128,128]{3,2,0,1:T(8,128)(2,1)}), bf16[1,336,128,128]{3,2,0,1:T(8,128)(2,1)}) %all-gather.17.cloned.1.call-update) | async-done | bytes 11010064 | tf_op jit(solution)/shard_map/all_gather | solution.py:63
  324.6 18.1 %fusion.21 = bf16[56,8,128,128]{3,1,2,0:T(8,128)(2,1)} fusion(bf16[42,8,128,128]{3,2,1,0:T(8,128)(2,1)} %bitcast.108, s32[336]{0:T(512)S(1)} %get-tuple-element.7, pred[336]{0:T(512)(128)(4,1)S(1)} %iota_compare_fusion.3), kind=kOutput, calls=%fused_computation.20 | convolution fusion | flops 4940443648 | bytes 25691792 | tf_op jit(solution)/shard_map/dot_general | solution.py:17
  342.7 8.8 %copy.25 = bf16[56,8,128,128]{3,2,1,0:T(8,128)(2,1)S(1)} copy(bf16[56,8,128,128]{3,1,2,0:T(8,128)(2,1)} %fusion.21) | data formatting | bytes 29360128
  351.5 10.5 %copy.17 = bf16[7,64,128,128]{3,1,2,0:T(8,128)(2,1)} copy(bf16[7,64,128,128]{3,2,1,0:T(8,128)(2,1)S(1)} %bitcast.104) | data formatting | bytes 29360128 | tf_op jit(solution)/shard_map/reshape | solution.py:24
  362.0 48.3 %all-gather.11.cloned.1.call-done = bf16[256,8192]{1,0:T(8,128)(2,1)} async-done(((bf16[8,8192]{1,0:T(8,128)(2,1)}), bf16[256,8192]{1,0:T(8,128)(2,1)}) %all-gather.11.cloned.1.call-update) | async-done | bytes 4194320 | tf_op jit(solution)/shard_map/all_gather | solution.py:44
  410.4 16.1 %fusion.24 = f32[256,896]{0,1:T(8,128)S(1)} fusion(bf16[256,8192]{1,0:T(8,128)(2,1)} %all-gather.11.cloned.1.call-done, bf16[112,8,64,128]{3,2,1,0:T(8,128)(2,1)} %bitcast.105), kind=kOutput, calls=%fused_computation.21 | convolution fusion | flops 3758096384 | bytes 19791872 | tf_op jit(solution)/shard_map/dot_general | solution.py:52
  426.5 40.7 %fusion = f32[256,8192]{1,0:T(8,128)} fusion(bf16[112,8,64,128]{3,2,1,0:T(8,128)(2,1)} %bitcast.107, bf16[256,8192]{1,0:T(8,128)(2,1)} %all-gather.11.cloned.1.call-done, bf16[112,8,64,128]{3,2,1,0:T(8,128)(2,1)} %bitcast.106, f32[256,896]{0,1:T(8,128)S(1)} %fusion.24), kind=kOutput, calls=%fused_computation.3 | convolution fusion | flops 7517569024 | bytes 42860544 | tf_op jit(solution)/shard_map/dot_general | solution.py:67
  467.2 0.0 reduce-scatter.2.cloned.1.call-update
  467.2 201.8 %reduce-scatter.2.cloned.1.call-done = f32[8,8192]{1,0:T(8,128)} async-done(((f32[256,8192]{1,0:T(8,128)}), f32[8,8192]{1,0:T(8,128)}) %reduce-scatter.2.cloned.1.call-update) | async-done | bytes 262160 | tf_op jit(solution)/shard_map/reduce_scatter | solution.py:72
  669.1 1.6 convert_element_type.31
  (3 shorter events, 0.0 us)
Async XLA Ops:
  6.5 106.5 %all-gather.13.cloned.1.call-start = ((), (), s32[]{:S(2)}) async-start(), calls=%async_computation.3 | async-start | bytes 13762560 | tf_op jit(solution)/shard_map/all_gather | solution.py:45
  7.3 211.6 %all-gather.15.cloned.1.call-start = ((), (), s32[]{:S(2)}) async-start(), calls=%async_computation.4 | async-start | bytes 13762560 | tf_op jit(solution)/shard_map/all_gather | solution.py:47
  8.0 316.6 %all-gather.17.cloned.1.call-start = ((), (), s32[]{:S(2)}) async-start(), calls=%async_computation.5 | async-start | bytes 13762560 | tf_op jit(solution)/shard_map/all_gather | solution.py:63
  8.7 401.6 %all-gather.11.cloned.1.call-start = ((), (), s32[]{:S(2)}) async-start(), calls=%async_computation.1 | async-start | bytes 4325376 | tf_op jit(solution)/shard_map/all_gather | solution.py:44
  9.3 659.8 %reduce-scatter.2.cloned.1.call-start = ((), (), s32[]{:S(2)}) async-start(), calls=%async_computation.2 | async-start | bytes 8650752 | tf_op jit(solution)/shard_map/reduce_scatter | solution.py:72
Sparse Core Ops, SparseCore 0:
  9.0 104.0 all-gather.12
  114.7 104.0 all-gather.14
  220.5 104.0 all-gather.16
  327.5 82.7 all-gather.10
  467.4 201.6 reduce-scatter.1
where the time goes:
time: 685 us; the launch traced here: 677 us
  waiting for transfers between devices  447 us (65%)
  matrix products  113 us (16%)
  local copies, waits for them, and re-layouts  94.5 us (14%)
  between operations  14.1 us (2%)
    reduce_scatter x1, waiting for transfers between devices, on_device(): lax.psum_scatter(partial_value, 'tensor', scatter_dimension=0, tiled=True)  202 us
    all_gather x1, waiting for transfers between devices, on_device(): part_gate = lax.all_gather(gate_values, 'seq', axis=0, tiled=True)  91 us
    dot_general x3, matrix products, place_blocks(): lax.dot_general(one_hot, flattened, (((0,), (0,)), ((), ())), preferred_e...  55.8 us
    all_gather x1, waiting for transfers between devices, on_device(): part_up = lax.all_gather(up_values, 'seq', axis=0, tiled=True)  52 us
    all_gather x1, waiting for transfers between devices, on_device(): part_down = lax.all_gather(down_values, 'seq', axis=0, tiled=True)  51.6 us
    reshape x3, local copies, waits for them, and re-layouts, arrange_blocks(): shaped = placed.reshape(outer_count, inner_count, block_size, block_size)  51.1 us
    all_gather x1, waiting for transfers between devices, on_device(): span_rows = lax.all_gather(tokens, 'tensor', axis=0, tiled=True)  48.3 us
    unnamed x10, local copies, waits for them, and re-layouts  41.9 us
  transfers between devices with their start and end apart: 5, of which 5 were waited for; matrix products, arithmetic and copies ran while one was open for 22% of the time, Pallas kernels for 0%

commit v1 on v0

v1 whole, which is shorter than its diff:
```python
import jax
import jax.numpy as jnp
from jax import lax
from jax.experimental import pallas as pl
from jax.experimental.pallas import tpu as pltpu
from jax.sharding import PartitionSpec as P

MESH = pl.DeviceIdType.MESH
BF16, F32 = jnp.bfloat16, jnp.float32
BLK = 128
TILE = 256
COLS = 7
OWN = 84
NONE = 2 * OWN
TILES = (11, 11, 10)
FIRST = (0, 11, 22)
AXES = (("y", "x", "z"), ("x", "z", "y"), ("z", "y", "x"))
GATHER_CUTS = ((0, 7, 11), (0, 7, 11), (0, 6, 10))
SCATTER_CUTS = ((0, 7, 11), (0, 7, 11), (0, 6, 10))
CHUNKS = 2


def group_index(part, z, x, y):
    at = {"z": z, "x": x, "y": y}
    d1, d2, d3 = AXES[part]
    return (at[d3] * 4 + at[d2]) * 4 + at[d1]


def kernel(
    tok, gate_in, gate_slots, up_in, up_slots, down_in, down_slots, counts, out,
    gate_w, up_w, down_w, first, xs, acc, esend, erecv, hid, r1, s2, r2, s3, r3, tab_v, tab_o, tab,
    w_sem, w_send, w_recv, t_send, t_recv, t_sem, a1s, a1r, a2s, a2r, a3s, a3r, es, er, hs, hr,
    b1s, b1r, b2s, b2r, b3s, b3r,
):
    s, t = lax.axis_index("seq"), lax.axis_index("tensor")
    yl, core = lax.div(s, 2), lax.rem(s, 2)
    z, x, yh = lax.div(t, 8), lax.rem(lax.div(t, 2), 4), lax.rem(t, 2)
    here = {"z": z, "x": x, "y": yh * 2 + yl, "core": core}

    def device(**moved):
        c = {**here, **moved}
        return (lax.rem(c["y"], 2) * 2 + c["core"], c["z"] * 8 + c["x"] * 2 + lax.div(c["y"], 2))

    def along(axis, off):
        return device(**{axis: lax.rem(here[axis] + off, 4)})

    mate = device(core=1 - core)
    pair = device(y=yh * 2 + (1 - yl))

    def remote(src, dst, send, recv, dev):
        return pltpu.make_async_remote_copy(
            src_ref=src, dst_ref=dst, send_sem=send, recv_sem=recv, device_id=dev, device_id_type=MESH
        )

    barrier = pltpu.get_barrier_semaphore()
    for dev in [mate] + [along(a, o) for a in "xyz" for o in (1, 2, 3)]:
        pl.semaphore_signal(barrier, inc=1, device_id=dev, device_id_type=MESH)
    pl.semaphore_wait(barrier, 10)

    gather1 = []
    for p in range(3):
        d1 = AXES[p][0]
        cols = pl.ds(FIRST[p] * TILE, TILES[p] * TILE)
        for o in (1, 2, 3):
            c = remote(tok.at[:, cols], first[p].at[here[d1]], a1s.at[p, o - 1], a1r.at[p, o - 1], along(d1, o))
            c.start()
            gather1.append(c)
    weights = ((gate_in, gate_w), (up_in, up_w), (down_in, down_w))
    local, swap = [], []
    for m, (src, dst) in enumerate(weights):
        local.append(pltpu.make_async_copy(src.at[0], dst.at[pl.ds(0, OWN)], w_sem.at[m]))
        swap.append(remote(src.at[0], dst.at[pl.ds(OWN, OWN)], w_send.at[m], w_recv.at[m], mate))
        local[m].start()
        swap[m].start()
        dst[NONE] = jnp.zeros((BLK, BLK), BF16)

    places = lax.broadcasted_iota(jnp.int32, (8, 128), 0) * 128 + lax.broadcasted_iota(jnp.int32, (8, 128), 1)
    for m, slots in enumerate((gate_slots, up_slots, down_slots)):
        live = counts[0, m] - s * OWN

        def enter(j, table, m=m, slots=slots, live=live):
            i = slots[0, j]
            if m < 2:
                place = lax.rem(i, COLS) * 128 + lax.div(i, COLS)
            else:
                place = lax.div(i, 64) * 128 + lax.rem(i, 64)
            return jnp.where((places == place) & (j < live), j, table)

        tab_v[m] = lax.fori_loop(0, OWN, enter, jnp.full((8, 128), NONE, jnp.int32))
    swap_tab = remote(tab_v, tab_o, t_send.at[0], t_recv.at[0], mate)
    swap_tab.start()

    for p in range(3):
        first[p][here[AXES[p][0]]] = tok[:, FIRST[p] * TILE : (FIRST[p] + TILES[p]) * TILE]

    gather2, gather3 = {}, {}
    for p in range(3):
        d1, d2, d3 = AXES[p]
        for o in range(3):
            gather1[p * 3 + o].wait_recv()

        def regroup(n, _, p=p, d2=d2, d3=d3):
            cols = pl.ds(pl.multiple_of(n * TILE, TILE), TILE)
            rows = [first[p][q, :, cols].astype(F32) for q in range(4)]
            xs[p][n, here[d3], here[d2]] = jnp.concatenate(rows, 0).astype(BF16)
            return 0

        lax.fori_loop(0, TILES[p], regroup, 0)
        for h in range(CHUNKS):
            a, b = GATHER_CUTS[p][h : h + 2]
            part = xs[p].at[pl.ds(a, b - a), here[d3], here[d2]]
            for o in (1, 2, 3):
                c = remote(part, part, a2s.at[h, p, o - 1], a2r.at[h, p, o - 1], along(d2, o))
                c.start()
                gather2[h, p, o] = c
    for h in range(CHUNKS):
        for p in range(3):
            d3 = AXES[p][2]
            a, b = GATHER_CUTS[p][h : h + 2]
            part = xs[p].at[pl.ds(a, b - a), here[d3]]
            for o in (1, 2, 3):
                gather2[h, p, o].wait_recv()
            for o in (1, 2, 3):
                c = remote(part, part, a3s.at[h, p, o - 1], a3r.at[h, p, o - 1], along(d3, o))
                c.start()
                gather3[h, p, o] = c

    swap_tab.wait()
    tab_v[...] = jnp.minimum(tab_v[...], tab_o[...] + OWN)
    to_scalar = pltpu.make_async_copy(tab_v, tab, t_sem.at[0])
    to_scalar.start()
    to_scalar.wait()
    for m in range(3):
        local[m].wait()
        swap[m].wait()

    def project(p, h, j):
        a, b = GATHER_CUTS[p][h : h + 2]
        left = jnp.concatenate([xs[p][n].reshape(512, TILE) for n in range(a, b)], 1)
        rows = []
        for r in range(2 * (FIRST[p] + a), 2 * (FIRST[p] + b)):
            rows.append(jnp.concatenate([gate_w[tab[0, j, r]], up_w[tab[1, j, r]]], 1))
        return jnp.dot(left, jnp.concatenate(rows, 0), preferred_element_type=F32).reshape(64, 8, TILE)

    def sums(j, zz, xx):
        rows = []
        for yy in range(4):
            v = acc[j, 0, group_index(0, zz, xx, yy)]
            v = v + acc[j, 1, group_index(1, zz, xx, yy)]
            rows.append(v + acc[j, 2, group_index(2, zz, xx, yy)])
        return jnp.concatenate(rows, 0)

    for p in range(3):
        for o in (1, 2, 3):
            gather3[0, p, o].wait_recv()

    def project0(j, _):
        for p in range(3):
            acc[j, p] = project(p, 0, j)
        return 0

    lax.fori_loop(0, COLS, project0, 0)
    for p in range(3):
        for o in (1, 2, 3):
            gather3[1, p, o].wait_recv()

    def exchange(j):
        return remote(esend.at[j], erecv.at[j], es.at[j], er.at[j], pair)

    def project1(j, _):
        for p in range(3):
            acc[j, p] = acc[j, p] + project(p, 1, j)

        def fill(i, _):
            zz = lax.div(i, 4)
            esend[j, i] = sums(j, (1 - yl) * 2 + zz, lax.rem(i, 4)).astype(BF16)
            return 0

        lax.fori_loop(0, 8, fill, 0)
        exchange(j).start()
        return 0

    lax.fori_loop(0, COLS, project1, 0)

    def give(j):
        mine = hid.at[0, j, pl.ds(yl * 8, 8)]
        return remote(mine, mine, hs.at[j], hr.at[j], pair)

    def finish(j, _):
        exchange(j).wait_recv()

        def rows(i, _):
            zz = lax.div(i, 4)
            v = sums(j, yl * 2 + zz, lax.rem(i, 4)) + erecv[j, i].astype(F32)
            g, u = v[:, :BLK], v[:, BLK:]
            hid[0, j, yl * 8 + i] = (g / (1.0 + jnp.exp(-g)) * u).astype(BF16)
            return 0

        lax.fori_loop(0, 8, rows, 0)
        give(j).start()
        return 0

    lax.fori_loop(0, COLS, finish, 0)

    def reorder(j, _):
        give(j).wait_recv()
        groups = hid[0, j].astype(F32).reshape(512, BLK)
        for p in (1, 2):
            order = [None] * 64
            for zz in range(4):
                for xx in range(4):
                    for yy in range(4):
                        g = (zz * 4 + xx) * 4 + yy
                        order[group_index(p, zz, xx, yy)] = groups[g * 8 : g * 8 + 8]
            hid[p, j] = jnp.concatenate(order, 0).reshape(16, 32, BLK).astype(BF16)
        return 0

    lax.fori_loop(0, COLS, reorder, 0)
    for c in gather1 + list(gather2.values()) + list(gather3.values()):
        c.wait_send()

    scatter1 = {}
    for h in range(CHUNKS):
        for p in range(3):
            d3 = AXES[p][2]
            a, b = SCATTER_CUTS[p][h : h + 2]

            def down(n, _, p=p):
                left = jnp.concatenate([hid[p, j].reshape(512, BLK) for j in range(COLS)], 1)
                col = 2 * (FIRST[p] + n)
                rows = []
                for j in range(COLS):
                    rows.append(jnp.concatenate([down_w[tab[2, j, col]], down_w[tab[2, j, col + 1]]], 1))
                v = jnp.dot(left, jnp.concatenate(rows, 0), preferred_element_type=F32)
                xs[p][n] = v.astype(BF16).reshape(4, 4, 32, TILE)
                return 0

            lax.fori_loop(a, b, down, 0)
            for o in (1, 2, 3):
                src = xs[p].at[pl.ds(a, b - a), lax.rem(here[d3] + o, 4)]
                c = remote(
                    src, r1[p].at[o - 1, pl.ds(a, b - a)], b1s.at[h, p, o - 1], b1r.at[h, p, o - 1], along(d3, o)
                )
                c.start()
                scatter1[h, p, o] = c
    scatter2 = {}
    for h in range(CHUNKS):
        for p in range(3):
            d2, d3 = AXES[p][1:]
            a, b = SCATTER_CUTS[p][h : h + 2]
            for o in (1, 2, 3):
                scatter1[h, p, o].wait_recv()

            def add1(n, _, p=p, d3=d3):
                v = xs[p][n, here[d3]].astype(F32)
                for o in range(3):
                    v = v + r1[p][o, n].astype(F32)
                s2[p][n] = v.astype(BF16)
                return 0

            lax.fori_loop(a, b, add1, 0)
            for o in (1, 2, 3):
                src = s2[p].at[pl.ds(a, b - a), lax.rem(here[d2] + o, 4)]
                c = remote(
                    src, r2[p].at[o - 1, pl.ds(a, b - a)], b2s.at[h, p, o - 1], b2r.at[h, p, o - 1], along(d2, o)
                )
                c.start()
                scatter2[h, p, o] = c
    scatter3 = {}
    for h in range(CHUNKS):
        for p in range(3):
            d1, d2 = AXES[p][:2]
            a, b = SCATTER_CUTS[p][h : h + 2]
            for o in (1, 2, 3):
                scatter2[h, p, o].wait_recv()

            def add2(n, _, p=p, d2=d2):
                v = s2[p][n, here[d2]].astype(F32)
                for o in range(3):
                    v = v + r2[p][o, n].astype(F32)
                s3[p][n] = v.reshape(4, 8, TILE)
                return 0

            lax.fori_loop(a, b, add2, 0)
            for o in (1, 2, 3):
                src = s3[p].at[pl.ds(a, b - a), lax.rem(here[d1] + o, 4)]
                c = remote(
                    src, r3[p].at[o - 1, pl.ds(a, b - a)], b3s.at[h, p, o - 1], b3r.at[h, p, o - 1], along(d1, o)
                )
                c.start()
                scatter3[h, p, o] = c
    for h in range(CHUNKS):
        for p in range(3):
            d1 = AXES[p][0]
            a, b = SCATTER_CUTS[p][h : h + 2]
            for o in (1, 2, 3):
                scatter3[h, p, o].wait_recv()

            def add3(n, _, p=p, d1=d1):
                v = s3[p][n, here[d1]] + r3[p][0, n] + r3[p][1, n] + r3[p][2, n]
                out[:, pl.ds(pl.multiple_of((FIRST[p] + n) * TILE, TILE), TILE)] = v.astype(BF16)
                return 0

            lax.fori_loop(a, b, add3, 0)

    def sent(j, _):
        exchange(j).wait_send()
        give(j).wait_send()
        return 0

    lax.fori_loop(0, COLS, sent, 0)
    for c in list(scatter1.values()) + list(scatter2.values()) + list(scatter3.values()):
        c.wait_send()


def on_device(tokens, gate_blocks, gate_slots, up_blocks, up_slots, down_blocks, down_slots, block_counts):
    vmem = pl.BlockSpec(memory_space=pltpu.VMEM)
    smem = pl.BlockSpec(memory_space=pltpu.SMEM)
    hbm = pl.BlockSpec(memory_space=pl.ANY)
    dma = pltpu.SemaphoreType.DMA

    def parts(shape, dtype):
        return [pltpu.VMEM(shape(n), dtype) for n in TILES]

    weights = pltpu.VMEM((NONE + 1, BLK, BLK), BF16)
    stage = dma((CHUNKS, 3, 3))
    return pl.pallas_call(
        kernel,
        name="layer",
        out_shape=jax.ShapeDtypeStruct(tokens.shape, BF16),
        in_specs=[vmem, hbm, smem, hbm, smem, hbm, smem, smem],
        out_specs=vmem,
        scratch_shapes=[
            weights,
            weights,
            weights,
            parts(lambda n: (4, 8, n * TILE), BF16),
            parts(lambda n: (n, 4, 4, 32, TILE), BF16),
            pltpu.VMEM((COLS, 3, 64, 8, TILE), F32),
            pltpu.VMEM((COLS, 8, 32, TILE), BF16),
            pltpu.VMEM((COLS, 8, 32, TILE), BF16),
            pltpu.VMEM((3, COLS, 16, 32, BLK), BF16),
            parts(lambda n: (3, n, 4, 32, TILE), BF16),
            parts(lambda n: (n, 4, 32, TILE), BF16),
            parts(lambda n: (3, n, 32, TILE), BF16),
            parts(lambda n: (n, 4, 8, TILE), F32),
            parts(lambda n: (3, n, 8, TILE), F32),
            pltpu.VMEM((3, 8, 128), jnp.int32),
            pltpu.VMEM((3, 8, 128), jnp.int32),
            pltpu.SMEM((3, 8, 128), jnp.int32),
            dma((3,)),
            dma((3,)),
            dma((3,)),
            dma((1,)),
            dma((1,)),
            dma((1,)),
            dma((3, 3)),
            dma((3, 3)),
            stage,
            stage,
            stage,
            stage,
            dma((COLS,)),
            dma((COLS,)),
            dma((COLS,)),
            dma((COLS,)),
            stage,
            stage,
            stage,
            stage,
            stage,
            stage,
        ],
        compiler_params=pltpu.CompilerParams(
            collective_id=0, has_side_effects=True, vmem_limit_bytes=60 * 2**20
        ),
    )(tokens, gate_blocks, gate_slots, up_blocks, up_slots, down_blocks, down_slots, block_counts)


def solution(mesh):
    return jax.shard_map(
        on_device,
        mesh=mesh,
        in_specs=(
            P(("seq", "tensor"), None),
            P("tensor", "seq", None, None),
            P("tensor", "seq"),
            P("tensor", "seq", None, None),
            P("tensor", "seq"),
            P("tensor", "seq", None, None),
            P("tensor", "seq"),
            P("tensor", None),
        ),
        out_specs=P(("seq", "tensor"), None),
        check_vma=False,
    )
```

time: 685 us -> 145 us (0.21); the launches traced: 677 us -> 144 us
  waiting for transfers between devices: 447 us -> 0 us
  Pallas kernels: 0 us -> 143 us
  matrix products: 113 us -> 0 us
  local copies, waits for them, and re-layouts: 94.5 us -> 1.57 us
  between operations: 14.1 us -> 0.01 us
    all_gather x4 -> x0, waiting for transfers between devices: 243 us -> none  [the longest x1 91 us: on_device(): part_gate = lax.all_gather(gate_values, 'seq', axis=0, tiled=True)]
    reduce_scatter x1 -> x0, waiting for transfers between devices: 202 us -> none  [on_device(): lax.psum_scatter(partial_value, 'tensor', scatter_dimension=0, tiled=True)]
    pallas_call x0 -> x1, Pallas kernels: none -> 143 us  [on_device(): pl.pallas_call(kernel, name='layer', out_shape=jax.ShapeDtypeStruct(token...]
    dot_general x5 -> x0, matrix products: 113 us -> none  [the longest x3 55.8 us: place_blocks(): lax.dot_general(one_hot, flattened, (((0,), (0,)), ((), ())), preferred_e...]
    reshape x3 -> x0, local copies, waits for them, and re-layouts: 51.1 us -> none  [arrange_blocks(): shaped = placed.reshape(outer_count, inner_count, block_size, block_size)]
    unnamed x10 -> x1, local copies, waits for them, and re-layouts: 41.9 us -> 1.57 us
  transfers between devices with their start and end apart: 5 -> 0, of which waited for: 5 -> 0; matrix products, arithmetic and copies ran while one was open for 22% -> 0% of each run, Pallas kernels for 0% -> 0%
where the time goes in v1:
time: 145 us; the launch traced here: 144 us
  Pallas kernels  143 us (99%)
  local copies, waits for them, and re-layouts  1.57 us (1%)
    pallas_call x1, Pallas kernels, on_device(): pl.pallas_call(kernel, name='layer', out_shape=jax.ShapeDtypeStruct(token...  143 us

profile of v1, /device:TPU:0, one launch (start us, length us, event | category | flops | bytes accessed | tf_op | source)
XLA Modules:
  0.0 144.4 jit_solution(14136175532962363741)
XLA Ops:
  0.0 142.8 %layer.1 = bf16[8,8192]{1,0:T(8,128)(2,1)} custom-call(bf16[8,8192]{1,0:T(8,128)(2,1)} %tok.1, bf16[1,84,128,128]{3,2,1,0:T(8,128)(2,1)} %gate_in.1, s32[1,84]{1,0:T(1,128)} %gate_slots.1, bf16[1,84,128,128]{3,2,1,0:T(8,128)(2,1)} %up_in.1, s32[1,84]{1,0:T(1,128)} %up_slots.1, bf16[1,84,128,128]{3,2,1,0:T(8,128)(2,1)} %down_in.1, s32[1,84]{1,0:T(1,128)} %down_slots.1, ...), custom_call_target="tpu_custom_call" | custom-call | tf_op jit(solution)/shard_map/layer/pallas_call | solution.py:327
  142.8 1.6 %copy.10 = bf16[8,8192]{1,0:T(8,128)(2,1)} copy(bf16[8,8192]{1,0:T(8,128)(2,1)} %layer.1) | data formatting | bytes 262144

commit v2 on v0

v2 whole, which is shorter than its diff:
```python
import jax
import jax.numpy as jnp
from jax import lax
from jax.experimental import pallas as pl
from jax.experimental.pallas import tpu as pltpu
from jax.sharding import PartitionSpec as P

MESH = pl.DeviceIdType.MESH
BF16, F32 = jnp.bfloat16, jnp.float32
BLK = 128
TILE = 256
COLS = 7
OWN = 84
NONE = 2 * OWN
TILES = (12, 8, 12)
FIRST = (0, TILES[0], TILES[0] + TILES[1])
AXES = (("y", "x", "z"), ("x", "z", "y"), ("z", "y", "x"))
PARTS = range(3)
HALVES = 2
CHUNKS = 2
CUTS = tuple((0, n // 2, n) for n in TILES)


def swap4(a, b):
    low = lax.broadcasted_iota(jnp.int32, a.shape, 0) < 4
    return jnp.where(low, a, pltpu.roll(b, 4, 0)), jnp.where(low, pltpu.roll(a, 4, 0), b)


def kernel(
    tok, gate_in, gate_slots, up_in, up_slots, down_in, down_slots, counts, out,
    gate_w, up_w, down_w, first, xs, acc, esend, erecv, hid, r0, r1, s2, r2, s3, r3, tab_v, tab_o, tab,
    w_sem, w_send, w_recv, t_send, t_recv, t_sem, a1s, a1r, a2s, a2r, a3s, a3r, a4s, a4r, es, er, hs, hr,
    b0s, b0r, b1s, b1r, b2s, b2r, b3s, b3r,
):
    s, t = lax.axis_index("seq"), lax.axis_index("tensor")
    yl, core = lax.div(s, 2), lax.rem(s, 2)
    z, x, yh = lax.div(t, 8), lax.rem(lax.div(t, 2), 4), lax.rem(t, 2)
    here = {"z": z, "x": x, "y": yh * 2 + yl, "core": core}

    def device(**moved):
        c = {**here, **moved}
        return (lax.rem(c["y"], 2) * 2 + c["core"], c["z"] * 8 + c["x"] * 2 + lax.div(c["y"], 2))

    def at(axis, off):
        return lax.rem(here[axis] + off, 4)

    def along(axis, off):
        return device(**{axis: at(axis, off)})

    mate = device(core=1 - core)
    pair = device(y=yh * 2 + (1 - yl))
    started = {}

    def remote(src, dst, send, recv, dev):
        return pltpu.make_async_remote_copy(
            src_ref=src, dst_ref=dst, send_sem=send, recv_sem=recv, device_id=dev, device_id_type=MESH
        )

    def start(*args):
        c = remote(*args)
        c.start()
        started[id(c)] = c
        return c

    barrier = pltpu.get_barrier_semaphore()
    for dev in [mate] + [along(a, o) for a in "xyz" for o in (1, 2, 3)]:
        pl.semaphore_signal(barrier, inc=1, device_id=dev, device_id_type=MESH)
    pl.semaphore_wait(barrier, 10)

    gather1, gather2, gather3, gather4 = {}, {}, {}, {}
    for p in PARTS:
        d1 = AXES[p][0]
        cols = pl.ds(FIRST[p] * TILE, TILES[p] * TILE)
        for o in (1, 2, 3):
            gather1[p, o] = start(
                tok.at[:, cols], first[p].at[here[d1]], a1s.at[p, o - 1], a1r.at[p, o - 1], along(d1, o)
            )
    weights = ((gate_in, gate_w), (up_in, up_w), (down_in, down_w))
    local, swap = [], []
    for m, (src, dst) in enumerate(weights):
        local.append(pltpu.make_async_copy(src.at[0], dst.at[pl.ds(0, OWN)], w_sem.at[m]))
        swap.append(remote(src.at[0], dst.at[pl.ds(OWN, OWN)], w_send.at[m], w_recv.at[m], mate))
        local[m].start()
        swap[m].start()
        dst[NONE] = jnp.zeros((BLK, BLK), BF16)

    places = lax.broadcasted_iota(jnp.int32, (8, 128), 0) * 128 + lax.broadcasted_iota(jnp.int32, (8, 128), 1)

    def tables():
        for m, slots in enumerate((gate_slots, up_slots, down_slots)):
            live = counts[0, m] - s * OWN

            def enter(j, table, m=m, slots=slots, live=live):
                i = slots[0, j]
                if m < 2:
                    place = lax.rem(i, COLS) * 128 + lax.div(i, COLS)
                else:
                    place = lax.div(i, 64) * 128 + lax.rem(i, 64)
                return jnp.where((places == place) & (j < live), j, table)

            tab_v[m] = lax.fori_loop(0, OWN, enter, jnp.full((8, 128), NONE, jnp.int32))

    for p in PARTS:
        first[p][here[AXES[p][0]]] = tok[:, FIRST[p] * TILE : (FIRST[p] + TILES[p]) * TILE]

    def start_gather2(h, p):
        d1, d2, d3 = AXES[p]
        part = xs[p].at[h, :, here[d3], here[d2]]
        for o in (1, 2, 3):
            gather2[h, p, o] = start(part, part, a2s.at[h, p, o - 1], a2r.at[h, p, o - 1], along(d2, o))

    for p in PARTS:
        d1, d2, d3 = AXES[p]
        for o in (1, 2, 3):
            gather1[p, o].wait_recv()

        def regroup(n, _, p=p, d2=d2, d3=d3):
            cols = pl.ds(pl.multiple_of(n * TILE, TILE), TILE)
            rows = [first[p][q, :, cols].astype(F32) for q in range(4)]
            top, end = swap4(rows[0], rows[1]), swap4(rows[2], rows[3])
            for h in range(HALVES):
                xs[p][h, n, here[d3], here[d2]] = jnp.concatenate([top[h], end[h]], 0).astype(BF16)
            return 0

        lax.fori_loop(0, TILES[p], regroup, 0)
        start_gather2(0, p)
    for p in PARTS:
        start_gather2(1, p)
    tables()
    swap_tab = remote(tab_v, tab_o, t_send.at[0], t_recv.at[0], mate)
    swap_tab.start()

    def start_gather3(h, p):
        d3 = AXES[p][2]
        for o in (1, 2, 3):
            gather2[h, p, o].wait_recv()
        part = xs[p].at[h, :, here[d3]]
        for i, o in enumerate((1, 3)):
            gather3[h, p, i] = start(part, part, a3s.at[h, p, i], a3r.at[h, p, i], along(d3, o))

    def start_gather4(h, p):
        d3 = AXES[p][2]
        for i, o in enumerate((1, 3)):
            gather3[h, p, i].wait_recv()
            part = xs[p].at[h, :, at(d3, 4 - o), pl.ds(2 * i, 2)]
            gather4[h, p, i] = start(part, part, a4s.at[h, p, i], a4r.at[h, p, i], along(d3, o))

    for p in PARTS:
        start_gather3(0, p)
    for p in PARTS:
        start_gather4(0, p)
    for p in PARTS:
        start_gather3(1, p)

    swap_tab.wait()
    tab_v[...] = jnp.minimum(tab_v[...], tab_o[...] + OWN)
    to_scalar = pltpu.make_async_copy(tab_v, tab, t_sem.at[0])
    to_scalar.start()
    to_scalar.wait()
    for m in range(3):
        local[m].wait()
        swap[m].wait()

    def project(p, h, j):
        left = jnp.concatenate([xs[p][h, n].reshape(256, TILE) for n in range(TILES[p])], 1)
        rows = []
        for r in range(2 * FIRST[p], 2 * (FIRST[p] + TILES[p])):
            rows.append(jnp.concatenate([gate_w[tab[0, j, r]], up_w[tab[1, j, r]]], 1))
        acc[j, p] = jnp.dot(left, jnp.concatenate(rows, 0), preferred_element_type=F32).reshape(32, 8, TILE)

    def sums(j, kz, kx):
        tiles = {}
        for ky in range(2):
            v = {}
            for i in range(2):
                zz, xx = 2 * kz + i, 2 * kx + i
                y0, y1 = (acc[j, 1, ((2 * ky + k) * 4 + zz) * 2 + kx] for k in range(2))
                v[1, i, 0], v[1, i, 1] = swap4(y0, y1)
                y0, y1 = (acc[j, 2, (xx * 4 + 2 * ky + k) * 2 + kz] for k in range(2))
                v[2, 0, i], v[2, 1, i] = swap4(y0, y1)
            for i in range(2):
                for k in range(2):
                    own = acc[j, 0, ((2 * kz + i) * 4 + 2 * kx + k) * 2 + ky]
                    tiles[i, k, ky] = own + v[1, i, k] + v[2, i, k]
        return {(i, k): jnp.concatenate([tiles[i, k, 0], tiles[i, k, 1]], 0) for i in range(2) for k in range(2)}

    def exchange(h, j):
        return remote(esend.at[h, j], erecv.at[h, j], es.at[h, j], er.at[h, j], pair)

    def give(h, j):
        mine = hid.at[h, 0, j, pl.ds(yl * 8, 8)]
        return remote(mine, mine, hs.at[h, j], hr.at[h, j], pair)

    def project_all(h, lo, hi):
        def body(j, _):
            for p in PARTS:
                project(p, h, j)
            for kx in range(2):
                for (i, k), v in sums(j, 1 - yl, kx).items():
                    esend[h, j, i * 4 + 2 * kx + k] = v.astype(BF16)
            exchange(h, j).start()
            return 0

        lax.fori_loop(lo, hi, body, 0)

    def finish(h):
        def body(j, _):
            exchange(h, j).wait_recv()
            for kx in range(2):
                for (i, k), v in sums(j, yl, kx).items():
                    row = i * 4 + 2 * kx + k
                    v = v + erecv[h, j, row].astype(F32)
                    g, u = v[:, :BLK], v[:, BLK:]
                    hid[h, 0, j, yl * 8 + row] = (g / (1.0 + jnp.exp(-g)) * u).astype(BF16)
            give(h, j).start()
            return 0

        lax.fori_loop(0, COLS, body, 0)

    def reorder(h):
        def body(j, _):
            give(h, j).wait_recv()
            v = hid[h, 0, j].astype(F32)

            def group(zz, xx, ky):
                return v[zz * 4 + xx, 8 * ky : 8 * ky + 8]

            for ky in range(2):
                for i in range(4):
                    a = [swap4(group(i, 2 * k, ky), group(i, 2 * k + 1, ky)) for k in range(2)]
                    b = [swap4(group(2 * k, i, ky), group(2 * k + 1, i, ky)) for k in range(2)]
                    for k in range(2):
                        yy = 2 * ky + k
                        hid[h, 1, j, yy * 4 + i] = jnp.concatenate([a[0][k], a[1][k]], 0).astype(BF16)
                        hid[h, 2, j, i * 4 + yy] = jnp.concatenate([b[0][k], b[1][k]], 0).astype(BF16)
            return 0

        lax.fori_loop(0, COLS, body, 0)

    scatter0, scatter1, scatter2, scatter3 = {}, {}, {}, {}

    def span(p, c):
        a, b = CUTS[p][c : c + 2]
        return a, b, pl.ds(a, b - a)

    def down(h, p, c):
        d3 = AXES[p][2]
        a, b, tiles = span(p, c)
        left = jnp.concatenate([hid[h, p, j].reshape(256, BLK) for j in range(COLS)], 1)
        for n in range(a, b):
            col = 2 * (FIRST[p] + n)
            rows = []
            for j in range(COLS):
                rows.append(jnp.concatenate([down_w[tab[2, j, col]], down_w[tab[2, j, col + 1]]], 1))
            v = jnp.dot(left, jnp.concatenate(rows, 0), preferred_element_type=F32)
            xs[p][h, n] = v.astype(BF16).reshape(4, 4, 16, TILE)
        for i, o in enumerate((1, 3)):
            src = xs[p].at[h, tiles, at(d3, 2), pl.ds(2 * i, 2)]
            scatter0[h, p, c, i] = start(
                src, r0[p].at[h, i, tiles], b0s.at[h, c, p, i], b0r.at[h, c, p, i], along(d3, o)
            )

    def pass_on(h, p, c):
        d3 = AXES[p][2]
        a, b, tiles = span(p, c)
        for i, o in enumerate((1, 3)):
            scatter0[h, p, c, i].wait_recv()

            def body(n, _, i=i, o=o):
                dst = xs[p].at[h, n, at(d3, o), pl.ds(2 * i, 2)]
                dst[...] = (dst[...].astype(F32) + r0[p][h, i, n].astype(F32)).astype(BF16)
                return 0

            lax.fori_loop(a, b, body, 0)
            src = xs[p].at[h, tiles, at(d3, o)]
            scatter1[h, p, c, i] = start(
                src, r1[p].at[h, i, tiles], b1s.at[h, c, p, i], b1r.at[h, c, p, i], along(d3, o)
            )

    def add1(h, p, c):
        d2, d3 = AXES[p][1:]
        a, b, tiles = span(p, c)
        for i in range(2):
            scatter1[h, p, c, i].wait_recv()

        def body(n, _):
            v = xs[p][h, n, here[d3]].astype(F32) + r1[p][h, 0, n].astype(F32) + r1[p][h, 1, n].astype(F32)
            s2[p][h, n] = v.astype(BF16)
            return 0

        lax.fori_loop(a, b, body, 0)
        for o in (1, 2, 3):
            src = s2[p].at[h, tiles, at(d2, o)]
            scatter2[h, p, c, o] = start(
                src, r2[p].at[h, o - 1, tiles], b2s.at[h, c, p, o - 1], b2r.at[h, c, p, o - 1], along(d2, o)
            )

    def sum2(h, p, n):
        v = s2[p][h, n, here[AXES[p][1]]].astype(F32)
        for o in range(3):
            v = v + r2[p][h, o, n].astype(F32)
        return v

    def add2(p, c):
        d1 = AXES[p][0]
        a, b, tiles = span(p, c)
        for h in range(HALVES):
            for o in (1, 2, 3):
                scatter2[h, p, c, o].wait_recv()

        def body(n, _):
            a, b = sum2(0, p, n), sum2(1, p, n)
            for k in range(2):
                u, v = swap4(a[8 * k : 8 * k + 8], b[8 * k : 8 * k + 8])
                s3[p][n, 2 * k] = u
                s3[p][n, 2 * k + 1] = v
            return 0

        lax.fori_loop(a, b, body, 0)
        for o in (1, 2, 3):
            src = s3[p].at[tiles, at(d1, o)]
            scatter3[p, c, o] = start(
                src, r3[p].at[o - 1, tiles], b3s.at[c, p, o - 1], b3r.at[c, p, o - 1], along(d1, o)
            )

    def add3(p, c):
        d1 = AXES[p][0]
        a, b, tiles = span(p, c)
        for o in (1, 2, 3):
            scatter3[p, c, o].wait_recv()

        def body(n, _):
            v = s3[p][n, here[d1]] + r3[p][0, n] + r3[p][1, n] + r3[p][2, n]
            out[:, pl.ds(pl.multiple_of((FIRST[p] + n) * TILE, TILE), TILE)] = v.astype(BF16)
            return 0

        lax.fori_loop(a, b, body, 0)

    def end_gather4(h):
        for p in PARTS:
            for i in range(2):
                gather4[h, p, i].wait_recv()

    def end_sends(h):
        for p in PARTS:
            for o in (1, 2, 3):
                done(gather2[h, p, o])
            for i in range(2):
                done(gather3[h, p, i])
                done(gather4[h, p, i])

    def done(c):
        c.wait_send()
        del started[id(c)]

    def each(step, *args):
        for c in range(CHUNKS):
            for p in PARTS:
                step(*args, p, c)

    end_gather4(0)
    project_all(0, 0, 4)
    for p in PARTS:
        start_gather4(1, p)
    project_all(0, 4, COLS)
    finish(0)
    end_gather4(1)
    project_all(1, 0, COLS)
    reorder(0)
    end_sends(0)
    each(down, 0)
    finish(1)
    each(pass_on, 0)
    reorder(1)
    end_sends(1)
    each(down, 1)
    each(add1, 0)
    each(pass_on, 1)
    each(add1, 1)
    each(add2)
    each(add3)

    def sent(j, _):
        for h in range(HALVES):
            exchange(h, j).wait_send()
            give(h, j).wait_send()
        return 0

    lax.fori_loop(0, COLS, sent, 0)
    for c in started.values():
        c.wait_send()


def on_device(tokens, gate_blocks, gate_slots, up_blocks, up_slots, down_blocks, down_slots, block_counts):
    vmem = pl.BlockSpec(memory_space=pltpu.VMEM)
    smem = pl.BlockSpec(memory_space=pltpu.SMEM)
    hbm = pl.BlockSpec(memory_space=pl.ANY)
    dma = pltpu.SemaphoreType.DMA

    def parts(shape, dtype):
        return [pltpu.VMEM(shape(n), dtype) for n in TILES]

    weights = pltpu.VMEM((NONE + 1, BLK, BLK), BF16)
    small, three, two, cols = dma((3,)), dma((HALVES, 3, 3)), dma((HALVES, 3, 2)), dma((HALVES, COLS))
    return pl.pallas_call(
        kernel,
        name="layer",
        out_shape=jax.ShapeDtypeStruct(tokens.shape, BF16),
        in_specs=[vmem, hbm, smem, hbm, smem, hbm, smem, smem],
        out_specs=vmem,
        scratch_shapes=[
            weights,
            weights,
            weights,
            parts(lambda n: (4, 8, n * TILE), BF16),
            parts(lambda n: (HALVES, n, 4, 4, 16, TILE), BF16),
            pltpu.VMEM((COLS, 3, 32, 8, TILE), F32),
            pltpu.VMEM((HALVES, COLS, 8, 16, TILE), BF16),
            pltpu.VMEM((HALVES, COLS, 8, 16, TILE), BF16),
            pltpu.VMEM((HALVES, 3, COLS, 16, 16, BLK), BF16),
            parts(lambda n: (HALVES, 2, n, 2, 16, TILE), BF16),
            parts(lambda n: (HALVES, 2, n, 4, 16, TILE), BF16),
            parts(lambda n: (HALVES, n, 4, 16, TILE), BF16),
            parts(lambda n: (HALVES, 3, n, 16, TILE), BF16),
            parts(lambda n: (n, 4, 8, TILE), F32),
            parts(lambda n: (3, n, 8, TILE), F32),
            pltpu.VMEM((3, 8, 128), jnp.int32),
            pltpu.VMEM((3, 8, 128), jnp.int32),
            pltpu.SMEM((3, 8, 128), jnp.int32),
            small, small, small, dma((1,)), dma((1,)), dma((1,)),
            dma((3, 3)), dma((3, 3)), three, three, two, two, two, two, cols, cols, cols, cols,
            dma((HALVES, CHUNKS, 3, 2)), dma((HALVES, CHUNKS, 3, 2)), dma((HALVES, CHUNKS, 3, 2)),
            dma((HALVES, CHUNKS, 3, 2)), dma((HALVES, CHUNKS, 3, 3)), dma((HALVES, CHUNKS, 3, 3)),
            dma((CHUNKS, 3, 3)), dma((CHUNKS, 3, 3)),
        ],
        compiler_params=pltpu.CompilerParams(
            collective_id=0, has_side_effects=True, vmem_limit_bytes=60 * 2**20
        ),
    )(tokens, gate_blocks, gate_slots, up_blocks, up_slots, down_blocks, down_slots, block_counts)


def solution(mesh):
    return jax.shard_map(
        on_device,
        mesh=mesh,
        in_specs=(
            P(("seq", "tensor"), None),
            P("tensor", "seq", None, None),
            P("tensor", "seq"),
            P("tensor", "seq", None, None),
            P("tensor", "seq"),
            P("tensor", "seq", None, None),
            P("tensor", "seq"),
            P("tensor", None),
        ),
        out_specs=P(("seq", "tensor"), None),
        check_vma=False,
    )
```

time: 685 us -> 114 us (0.17)
  waiting for transfers between devices: 447 us -> 0 us
  matrix products: 113 us -> 0 us
  Pallas kernels: 0 us -> 112 us
  local copies, waits for them, and re-layouts: 94.5 us -> 1.57 us
  between operations: 14.1 us -> 0.01 us
    all_gather x4 -> x0, waiting for transfers between devices: 243 us -> none  [the longest x1 91 us: on_device(): part_gate = lax.all_gather(gate_values, 'seq', axis=0, tiled=True)]
    reduce_scatter x1 -> x0, waiting for transfers between devices: 202 us -> none  [on_device(): lax.psum_scatter(partial_value, 'tensor', scatter_dimension=0, tiled=True)]
    dot_general x5 -> x0, matrix products: 113 us -> none  [the longest x3 55.8 us: place_blocks(): lax.dot_general(one_hot, flattened, (((0,), (0,)), ((), ())), preferred_e...]
    pallas_call x0 -> x1, Pallas kernels: none -> 112 us  [on_device(): pl.pallas_call(kernel, name='layer', out_shape=jax.ShapeDtypeStruct(token...]
    reshape x3 -> x0, local copies, waits for them, and re-layouts: 51.1 us -> none  [arrange_blocks(): shaped = placed.reshape(outer_count, inner_count, block_size, block_size)]
    unnamed x10 -> x1, local copies, waits for them, and re-layouts: 41.9 us -> 1.57 us
  transfers between devices with their start and end apart: 5 -> 0, of which waited for: 5 -> 0; matrix products, arithmetic and copies ran while one was open for 22% -> 0% of each run, Pallas kernels for 0% -> 0%
where the time goes in v2:
time: 114 us; the launch traced here: 113 us
  Pallas kernels  112 us (98%)
  local copies, waits for them, and re-layouts  1.57 us (1%)
    pallas_call x1, Pallas kernels, on_device(): pl.pallas_call(kernel, name='layer', out_shape=jax.ShapeDtypeStruct(token...  112 us

profile of v2, /device:TPU:0, one launch (start us, length us, event | category | flops | bytes accessed | tf_op | source)
XLA Modules:
  0.0 113.2 jit_solution(2878272420765655746)
XLA Ops:
  0.0 111.7 %layer.1 = bf16[8,8192]{1,0:T(8,128)(2,1)} custom-call(bf16[8,8192]{1,0:T(8,128)(2,1)} %tok.1, bf16[1,84,128,128]{3,2,1,0:T(8,128)(2,1)} %gate_in.1, s32[1,84]{1,0:T(1,128)} %gate_slots.1, bf16[1,84,128,128]{3,2,1,0:T(8,128)(2,1)} %up_in.1, s32[1,84]{1,0:T(1,128)} %up_slots.1, bf16[1,84,128,128]{3,2,1,0:T(8,128)(2,1)} %down_in.1, s32[1,84]{1,0:T(1,128)} %down_slots.1, ...), custom_call_target="tpu_custom_call" | custom-call | tf_op jit(solution)/shard_map/layer/pallas_call | solution.py:405
  111.7 1.6 %copy.10 = bf16[8,8192]{1,0:T(8,128)(2,1)} copy(bf16[8,8192]{1,0:T(8,128)(2,1)} %layer.1) | data formatting | bytes 262144

commit v3 on v2

--- a/solution.py
+++ b/solution.py
@@ -17,8 +17,8 @@
 AXES = (("y", "x", "z"), ("x", "z", "y"), ("z", "y", "x"))
 PARTS = range(3)
 HALVES = 2
-CHUNKS = 2
-CUTS = tuple((0, n // 2, n) for n in TILES)
+PIECES = ((0, 0, 6), (1, 12, 4), (2, 20, 6), (0, 6, 6), (1, 16, 4), (2, 26, 6))
+ALL = range(len(PIECES))
 
 
 def swap4(a, b):
@@ -28,9 +28,9 @@
 
 def kernel(
     tok, gate_in, gate_slots, up_in, up_slots, down_in, down_slots, counts, out,
-    gate_w, up_w, down_w, first, xs, acc, esend, erecv, hid, r0, r1, s2, r2, s3, r3, tab_v, tab_o, tab,
+    gate_w, up_w, down_w, first, xs, ys, acc, esend, erecv, hid, r0, r1, s2, r2, s3, r3, tab_v, tab_o, tab,
     w_sem, w_send, w_recv, t_send, t_recv, t_sem, a1s, a1r, a2s, a2r, a3s, a3r, a4s, a4r, es, er, hs, hr,
-    b0s, b0r, b1s, b1r, b2s, b2r, b3s, b3r,
+    b0s, b0r, b1s, b1r, b2s, b2r, b3s, b3r, b4s, b4r,
 ):
     s, t = lax.axis_index("seq"), lax.axis_index("tensor")
     yl, core = lax.div(s, 2), lax.rem(s, 2)
@@ -81,7 +81,8 @@
         local.append(pltpu.make_async_copy(src.at[0], dst.at[pl.ds(0, OWN)], w_sem.at[m]))
         swap.append(remote(src.at[0], dst.at[pl.ds(OWN, OWN)], w_send.at[m], w_recv.at[m], mate))
         local[m].start()
-        swap[m].start()
+        if m < 2:
+            swap[m].start()
         dst[NONE] = jnp.zeros((BLK, BLK), BF16)
 
     places = lax.broadcasted_iota(jnp.int32, (8, 128), 0) * 128 + lax.broadcasted_iota(jnp.int32, (8, 128), 1)
@@ -105,7 +106,7 @@
 
     def start_gather2(h, p):
         d1, d2, d3 = AXES[p]
-        part = xs[p].at[h, :, here[d3], here[d2]]
+        part = xs[p].at[h, here[d3], here[d2]]
         for o in (1, 2, 3):
             gather2[h, p, o] = start(part, part, a2s.at[h, p, o - 1], a2r.at[h, p, o - 1], along(d2, o))
 
@@ -119,7 +120,7 @@
             rows = [first[p][q, :, cols].astype(F32) for q in range(4)]
             top, end = swap4(rows[0], rows[1]), swap4(rows[2], rows[3])
             for h in range(HALVES):
-                xs[p][h, n, here[d3], here[d2]] = jnp.concatenate([top[h], end[h]], 0).astype(BF16)
+                xs[p][h, here[d3], here[d2], n] = jnp.concatenate([top[h], end[h]], 0).astype(BF16)
             return 0
 
         lax.fori_loop(0, TILES[p], regroup, 0)
@@ -134,15 +135,16 @@
         d3 = AXES[p][2]
         for o in (1, 2, 3):
             gather2[h, p, o].wait_recv()
-        part = xs[p].at[h, :, here[d3]]
-        for i, o in enumerate((1, 3)):
-            gather3[h, p, i] = start(part, part, a3s.at[h, p, i], a3r.at[h, p, i], along(d3, o))
+        for k in range(2):
+            for i, o in enumerate((1, 3)):
+                part = xs[p].at[h, here[d3], pl.ds(2 * (k if i == 0 else 1 - k), 2)]
+                gather3[h, p, i, k] = start(part, part, a3s.at[h, p, i, k], a3r.at[h, p, i, k], along(d3, o))
 
     def start_gather4(h, p):
         d3 = AXES[p][2]
         for i, o in enumerate((1, 3)):
-            gather3[h, p, i].wait_recv()
-            part = xs[p].at[h, :, at(d3, 4 - o), pl.ds(2 * i, 2)]
+            gather3[h, p, i, 0].wait_recv()
+            part = xs[p].at[h, at(d3, 4 - o), pl.ds(2 * i, 2)]
             gather4[h, p, i] = start(part, part, a4s.at[h, p, i], a4r.at[h, p, i], along(d3, o))
 
     for p in PARTS:
@@ -157,12 +159,12 @@
     to_scalar = pltpu.make_async_copy(tab_v, tab, t_sem.at[0])
     to_scalar.start()
     to_scalar.wait()
-    for m in range(3):
+    for m in range(2):
         local[m].wait()
         swap[m].wait()
 
     def project(p, h, j):
-        left = jnp.concatenate([xs[p][h, n].reshape(256, TILE) for n in range(TILES[p])], 1)
+        left = jnp.concatenate([xs[p][h, :, :, n].reshape(256, TILE) for n in range(TILES[p])], 1)
         rows = []
         for r in range(2 * FIRST[p], 2 * (FIRST[p] + TILES[p])):
             rows.append(jnp.concatenate([gate_w[tab[0, j, r]], up_w[tab[1, j, r]]], 1))
@@ -237,126 +239,114 @@
 
         lax.fori_loop(0, COLS, body, 0)
 
-    scatter0, scatter1, scatter2, scatter3 = {}, {}, {}, {}
-
-    def span(p, c):
-        a, b = CUTS[p][c : c + 2]
-        return a, b, pl.ds(a, b - a)
-
-    def down(h, p, c):
+    scatter0, scatter1, scatter2, scatter3, scatter4 = {}, {}, {}, {}, {}
+
+    def down(h, q):
+        p, a, tiles = PIECES[q]
         d3 = AXES[p][2]
-        a, b, tiles = span(p, c)
         left = jnp.concatenate([hid[h, p, j].reshape(256, BLK) for j in range(COLS)], 1)
-        for n in range(a, b):
-            col = 2 * (FIRST[p] + n)
+        for n in range(tiles):
+            col = 2 * (a + n)
             rows = []
             for j in range(COLS):
                 rows.append(jnp.concatenate([down_w[tab[2, j, col]], down_w[tab[2, j, col + 1]]], 1))
             v = jnp.dot(left, jnp.concatenate(rows, 0), preferred_element_type=F32)
-            xs[p][h, n] = v.astype(BF16).reshape(4, 4, 16, TILE)
+            ys[q][h, :, :, n] = v.astype(BF16).reshape(4, 4, 16, TILE)
         for i, o in enumerate((1, 3)):
-            src = xs[p].at[h, tiles, at(d3, 2), pl.ds(2 * i, 2)]
-            scatter0[h, p, c, i] = start(
-                src, r0[p].at[h, i, tiles], b0s.at[h, c, p, i], b0r.at[h, c, p, i], along(d3, o)
-            )
-
-    def pass_on(h, p, c):
+            src = ys[q].at[h, at(d3, 2), pl.ds(2 * i, 2)]
+            scatter0[h, q, i] = start(src, r0[q].at[h, i], b0s.at[h, q, i], b0r.at[h, q, i], along(d3, o))
+        for i, o in enumerate((1, 3)):
+            ready = pl.ds(2 - 2 * i, 2)
+            src = ys[q].at[h, at(d3, o), ready]
+            scatter4[h, q, i] = start(src, r1[q].at[h, i, ready], b4s.at[h, q, i], b4r.at[h, q, i], along(d3, o))
+
+    def pass_on(h, q):
+        p, a, tiles = PIECES[q]
         d3 = AXES[p][2]
-        a, b, tiles = span(p, c)
         for i, o in enumerate((1, 3)):
-            scatter0[h, p, c, i].wait_recv()
+            scatter0[h, q, i].wait_recv()
 
             def body(n, _, i=i, o=o):
-                dst = xs[p].at[h, n, at(d3, o), pl.ds(2 * i, 2)]
-                dst[...] = (dst[...].astype(F32) + r0[p][h, i, n].astype(F32)).astype(BF16)
+                for k in range(2):
+                    v = ys[q][h, at(d3, o), 2 * i + k, n].astype(F32) + r0[q][h, i, k, n].astype(F32)
+                    ys[q][h, at(d3, o), 2 * i + k, n] = v.astype(BF16)
                 return 0
 
-            lax.fori_loop(a, b, body, 0)
-            src = xs[p].at[h, tiles, at(d3, o)]
-            scatter1[h, p, c, i] = start(
-                src, r1[p].at[h, i, tiles], b1s.at[h, c, p, i], b1r.at[h, c, p, i], along(d3, o)
-            )
-
-    def add1(h, p, c):
-        d2, d3 = AXES[p][1:]
-        a, b, tiles = span(p, c)
+            lax.fori_loop(0, tiles, body, 0)
+            rest = pl.ds(2 * i, 2)
+            src = ys[q].at[h, at(d3, o), rest]
+            scatter1[h, q, i] = start(src, r1[q].at[h, i, rest], b1s.at[h, q, i], b1r.at[h, q, i], along(d3, o))
+
+    def sum1(h, q, k, n):
+        v = ys[q][h, here[AXES[PIECES[q][0]][2]], k, n].astype(F32)
+        return v + r1[q][h, 0, k, n].astype(F32) + r1[q][h, 1, k, n].astype(F32)
+
+    def add1(h, q):
+        p, a, tiles = PIECES[q]
+        d2 = AXES[p][1]
         for i in range(2):
-            scatter1[h, p, c, i].wait_recv()
+            scatter1[h, q, i].wait_recv()
+            scatter4[h, q, i].wait_recv()
 
         def body(n, _):
-            v = xs[p][h, n, here[d3]].astype(F32) + r1[p][h, 0, n].astype(F32) + r1[p][h, 1, n].astype(F32)
-            s2[p][h, n] = v.astype(BF16)
-            return 0
-
-        lax.fori_loop(a, b, body, 0)
-        for o in (1, 2, 3):
-            src = s2[p].at[h, tiles, at(d2, o)]
-            scatter2[h, p, c, o] = start(
-                src, r2[p].at[h, o - 1, tiles], b2s.at[h, c, p, o - 1], b2r.at[h, c, p, o - 1], along(d2, o)
-            )
-
-    def sum2(h, p, n):
-        v = s2[p][h, n, here[AXES[p][1]]].astype(F32)
+            for k in range(4):
+                s2[q][h, k, n] = sum1(h, q, k, n).astype(BF16)
+            return 0
+
+        lax.fori_loop(0, tiles, body, 0)
+        for o in (1, 2, 3):
+            src = s2[q].at[h, at(d2, o)]
+            scatter2[h, q, o] = start(src, r2[q].at[h, o - 1], b2s.at[h, q, o - 1], b2r.at[h, q, o - 1], along(d2, o))
+
+    def sum2(h, q, n):
+        v = sum1(h, q, here[AXES[PIECES[q][0]][1]], n)
         for o in range(3):
-            v = v + r2[p][h, o, n].astype(F32)
+            v = v + r2[q][h, o, n].astype(F32)
         return v
 
-    def add2(p, c):
+    def add2(h, q):
+        p, a, tiles = PIECES[q]
         d1 = AXES[p][0]
-        a, b, tiles = span(p, c)
+        for o in (1, 2, 3):
+            scatter2[h, q, o].wait_recv()
+
+        def body(n, _):
+            a, b = sum2(h, q, 2 * n), sum2(h, q, 2 * n + 1)
+            for k in range(2):
+                u, v = swap4(a[8 * k : 8 * k + 8], b[8 * k : 8 * k + 8])
+                s3[q][h, 2 * k, n] = u
+                s3[q][h, 2 * k + 1, n] = v
+            return 0
+
+        lax.fori_loop(0, tiles // 2, body, 0)
+        for o in (1, 2, 3):
+            src = s3[q].at[h, at(d1, o)]
+            scatter3[h, q, o] = start(src, r3[q].at[h, o - 1], b3s.at[h, q, o - 1], b3r.at[h, q, o - 1], along(d1, o))
+
+    def add3(q):
+        p, a, tiles = PIECES[q]
+        d1 = AXES[p][0]
         for h in range(HALVES):
             for o in (1, 2, 3):
-                scatter2[h, p, c, o].wait_recv()
+                scatter3[h, q, o].wait_recv()
 
         def body(n, _):
-            a, b = sum2(0, p, n), sum2(1, p, n)
-            for k in range(2):
-                u, v = swap4(a[8 * k : 8 * k + 8], b[8 * k : 8 * k + 8])
-                s3[p][n, 2 * k] = u
-                s3[p][n, 2 * k + 1] = v
-            return 0
-
-        lax.fori_loop(a, b, body, 0)
-        for o in (1, 2, 3):
-            src = s3[p].at[tiles, at(d1, o)]
-            scatter3[p, c, o] = start(
-                src, r3[p].at[o - 1, tiles], b3s.at[c, p, o - 1], b3r.at[c, p, o - 1], along(d1, o)
-            )
-
-    def add3(p, c):
-        d1 = AXES[p][0]
-        a, b, tiles = span(p, c)
-        for o in (1, 2, 3):
-            scatter3[p, c, o].wait_recv()
-
-        def body(n, _):
-            v = s3[p][n, here[d1]] + r3[p][0, n] + r3[p][1, n] + r3[p][2, n]
-            out[:, pl.ds(pl.multiple_of((FIRST[p] + n) * TILE, TILE), TILE)] = v.astype(BF16)
-            return 0
-
-        lax.fori_loop(a, b, body, 0)
+            v = [s3[q][h, here[d1], n] + r3[q][h, 0, n] + r3[q][h, 1, n] + r3[q][h, 2, n] for h in range(HALVES)]
+            for k, rows in enumerate(swap4(*v)):
+                out[:, pl.ds(pl.multiple_of((a + 2 * n + k) * TILE, TILE), TILE)] = rows.astype(BF16)
+            return 0
+
+        lax.fori_loop(0, tiles // 2, body, 0)
 
     def end_gather4(h):
         for p in PARTS:
             for i in range(2):
+                gather3[h, p, i, 1].wait_recv()
                 gather4[h, p, i].wait_recv()
 
-    def end_sends(h):
-        for p in PARTS:
-            for o in (1, 2, 3):
-                done(gather2[h, p, o])
-            for i in range(2):
-                done(gather3[h, p, i])
-                done(gather4[h, p, i])
-
-    def done(c):
-        c.wait_send()
-        del started[id(c)]
-
     def each(step, *args):
-        for c in range(CHUNKS):
-            for p in PARTS:
-                step(*args, p, c)
+        for q in ALL:
+            step(*args, q)
 
     end_gather4(0)
     project_all(0, 0, 4)
@@ -365,19 +355,21 @@
     project_all(0, 4, COLS)
     finish(0)
     end_gather4(1)
+    swap[2].start()
     project_all(1, 0, COLS)
     reorder(0)
-    end_sends(0)
+    local[2].wait()
+    swap[2].wait()
     each(down, 0)
     finish(1)
     each(pass_on, 0)
     reorder(1)
-    end_sends(1)
     each(down, 1)
+    each(pass_on, 1)
     each(add1, 0)
-    each(pass_on, 1)
     each(add1, 1)
-    each(add2)
+    each(add2, 0)
+    each(add2, 1)
     each(add3)
 
     def sent(j, _):
@@ -400,8 +392,13 @@
     def parts(shape, dtype):
         return [pltpu.VMEM(shape(n), dtype) for n in TILES]
 
+    def pieces(shape, dtype):
+        return [pltpu.VMEM(shape(n), dtype) for _, _, n in PIECES]
+
     weights = pltpu.VMEM((NONE + 1, BLK, BLK), BF16)
     small, three, two, cols = dma((3,)), dma((HALVES, 3, 3)), dma((HALVES, 3, 2)), dma((HALVES, COLS))
+    many = len(PIECES)
+    out_two, out_three = dma((HALVES, many, 2)), dma((HALVES, many, 3))
     return pl.pallas_call(
         kernel,
         name="layer",
@@ -413,25 +410,24 @@
             weights,
             weights,
             parts(lambda n: (4, 8, n * TILE), BF16),
-            parts(lambda n: (HALVES, n, 4, 4, 16, TILE), BF16),
+            parts(lambda n: (HALVES, 4, 4, n, 16, TILE), BF16),
+            pieces(lambda n: (HALVES, 4, 4, n, 16, TILE), BF16),
             pltpu.VMEM((COLS, 3, 32, 8, TILE), F32),
             pltpu.VMEM((HALVES, COLS, 8, 16, TILE), BF16),
             pltpu.VMEM((HALVES, COLS, 8, 16, TILE), BF16),
             pltpu.VMEM((HALVES, 3, COLS, 16, 16, BLK), BF16),
-            parts(lambda n: (HALVES, 2, n, 2, 16, TILE), BF16),
-            parts(lambda n: (HALVES, 2, n, 4, 16, TILE), BF16),
-            parts(lambda n: (HALVES, n, 4, 16, TILE), BF16),
-            parts(lambda n: (HALVES, 3, n, 16, TILE), BF16),
-            parts(lambda n: (n, 4, 8, TILE), F32),
-            parts(lambda n: (3, n, 8, TILE), F32),
+            pieces(lambda n: (HALVES, 2, 2, n, 16, TILE), BF16),
+            pieces(lambda n: (HALVES, 2, 4, n, 16, TILE), BF16),
+            pieces(lambda n: (HALVES, 4, n, 16, TILE), BF16),
+            pieces(lambda n: (HALVES, 3, n, 16, TILE), BF16),
+            pieces(lambda n: (HALVES, 4, n // 2, 8, TILE), F32),
+            pieces(lambda n: (HALVES, 3, n // 2, 8, TILE), F32),
             pltpu.VMEM((3, 8, 128), jnp.int32),
             pltpu.VMEM((3, 8, 128), jnp.int32),
             pltpu.SMEM((3, 8, 128), jnp.int32),
             small, small, small, dma((1,)), dma((1,)), dma((1,)),
-            dma((3, 3)), dma((3, 3)), three, three, two, two, two, two, cols, cols, cols, cols,
-            dma((HALVES, CHUNKS, 3, 2)), dma((HALVES, CHUNKS, 3, 2)), dma((HALVES, CHUNKS, 3, 2)),
-            dma((HALVES, CHUNKS, 3, 2)), dma((HALVES, CHUNKS, 3, 3)), dma((HALVES, CHUNKS, 3, 3)),
-            dma((CHUNKS, 3, 3)), dma((CHUNKS, 3, 3)),
+            dma((3, 3)), dma((3, 3)), three, three, dma((HALVES, 3, 2, 2)), dma((HALVES, 3, 2, 2)), two, two, cols, cols, cols, cols,
+            out_two, out_two, out_two, out_two, out_three, out_three, out_three, out_three, out_two, out_two,
         ],
         compiler_params=pltpu.CompilerParams(
             collective_id=0, has_side_effects=True, vmem_limit_bytes=60 * 2**20

time: 114 us -> 115 us (level)
    pallas_call x1, Pallas kernels: 112 us -> 113 us  [on_device(): pl.pallas_call(kernel, name='layer', out_shape=jax.ShapeDtypeStruct(token...]
where the time goes in v3:
time: 115 us
  Pallas kernels  113 us (98%)
  local copies, waits for them, and re-layouts  1.57 us (1%)
    pallas_call x1, Pallas kernels, on_device(): pl.pallas_call(kernel, name='layer', out_shape=jax.ShapeDtypeStruct(token...  113 us

profile of v3, /device:TPU:0, one launch (start us, length us, event | category | flops | bytes accessed | tf_op | source)
XLA Modules:
  0.0 114.7 jit_solution(7722179344368911578)
XLA Ops:
  0.0 113.2 %layer.1 = bf16[8,8192]{1,0:T(8,128)(2,1)} custom-call(bf16[8,8192]{1,0:T(8,128)(2,1)} %tok.1, bf16[1,84,128,128]{3,2,1,0:T(8,128)(2,1)} %gate_in.1, s32[1,84]{1,0:T(1,128)} %gate_slots.1, bf16[1,84,128,128]{3,2,1,0:T(8,128)(2,1)} %up_in.1, s32[1,84]{1,0:T(1,128)} %up_slots.1, bf16[1,84,128,128]{3,2,1,0:T(8,128)(2,1)} %down_in.1, s32[1,84]{1,0:T(1,128)} %down_slots.1, ...), custom_call_target="tpu_custom_call" | custom-call | tf_op jit(solution)/shard_map/layer/pallas_call | solution.py:402
  113.2 1.6 %copy.10 = bf16[8,8192]{1,0:T(8,128)(2,1)} copy(bf16[8,8192]{1,0:T(8,128)(2,1)} %layer.1) | data formatting | bytes 262144

commit v4 on v3

--- a/solution.py
+++ b/solution.py
@@ -27,10 +27,11 @@
 
 
 def kernel(
-    tok, gate_in, gate_slots, up_in, up_slots, down_in, down_slots, counts, out,
+    tok, gate_in, gate_slots_in, up_in, up_slots_in, down_in, down_slots_in, counts_in, out,
     gate_w, up_w, down_w, first, xs, ys, acc, esend, erecv, hid, r0, r1, s2, r2, s3, r3, tab_v, tab_o, tab,
     w_sem, w_send, w_recv, t_send, t_recv, t_sem, a1s, a1r, a2s, a2r, a3s, a3r, a4s, a4r, es, er, hs, hr,
     b0s, b0r, b1s, b1r, b2s, b2r, b3s, b3r, b4s, b4r,
+    gate_slots, up_slots, down_slots, counts, slot_sem, tok_sem,
 ):
     s, t = lax.axis_index("seq"), lax.axis_index("tensor")
     yl, core = lax.div(s, 2), lax.rem(s, 2)
@@ -65,6 +66,18 @@
     barrier = pltpu.get_barrier_semaphore()
     for dev in [mate] + [along(a, o) for a in "xyz" for o in (1, 2, 3)]:
         pl.semaphore_signal(barrier, inc=1, device_id=dev, device_id_type=MESH)
+    loads = []
+    for p in PARTS:
+        cols = pl.ds(FIRST[p] * TILE, TILES[p] * TILE)
+        loads.append(pltpu.make_async_copy(tok.at[:, cols], first[p].at[here[AXES[p][0]]], tok_sem.at[p]))
+    slot_loads = [
+        pltpu.make_async_copy(src, dst, slot_sem.at[i])
+        for i, (src, dst) in enumerate(
+            ((gate_slots_in, gate_slots), (up_slots_in, up_slots), (down_slots_in, down_slots), (counts_in, counts))
+        )
+    ]
+    for c in loads + slot_loads:
+        c.start()
     pl.semaphore_wait(barrier, 10)
 
     gather1, gather2, gather3, gather4 = {}, {}, {}, {}
@@ -101,9 +114,6 @@
 
             tab_v[m] = lax.fori_loop(0, OWN, enter, jnp.full((8, 128), NONE, jnp.int32))
 
-    for p in PARTS:
-        first[p][here[AXES[p][0]]] = tok[:, FIRST[p] * TILE : (FIRST[p] + TILES[p]) * TILE]
-
     def start_gather2(h, p):
         d1, d2, d3 = AXES[p]
         part = xs[p].at[h, here[d3], here[d2]]
@@ -114,6 +124,7 @@
         d1, d2, d3 = AXES[p]
         for o in (1, 2, 3):
             gather1[p, o].wait_recv()
+        loads[p].wait()
 
         def regroup(n, _, p=p, d2=d2, d3=d3):
             cols = pl.ds(pl.multiple_of(n * TILE, TILE), TILE)
@@ -127,6 +138,8 @@
         start_gather2(0, p)
     for p in PARTS:
         start_gather2(1, p)
+    for c in slot_loads:
+        c.wait()
     tables()
     swap_tab = remote(tab_v, tab_o, t_send.at[0], t_recv.at[0], mate)
     swap_tab.start()
@@ -349,10 +362,10 @@
             step(*args, q)
 
     end_gather4(0)
-    project_all(0, 0, 4)
+    project_all(0, 0, 2)
     for p in PARTS:
         start_gather4(1, p)
-    project_all(0, 4, COLS)
+    project_all(0, 2, COLS)
     finish(0)
     end_gather4(1)
     swap[2].start()
@@ -385,7 +398,6 @@
 
 def on_device(tokens, gate_blocks, gate_slots, up_blocks, up_slots, down_blocks, down_slots, block_counts):
     vmem = pl.BlockSpec(memory_space=pltpu.VMEM)
-    smem = pl.BlockSpec(memory_space=pltpu.SMEM)
     hbm = pl.BlockSpec(memory_space=pl.ANY)
     dma = pltpu.SemaphoreType.DMA
 
@@ -403,7 +415,7 @@
         kernel,
         name="layer",
         out_shape=jax.ShapeDtypeStruct(tokens.shape, BF16),
-        in_specs=[vmem, hbm, smem, hbm, smem, hbm, smem, smem],
+        in_specs=[hbm] * 8,
         out_specs=vmem,
         scratch_shapes=[
             weights,
@@ -428,6 +440,8 @@
             small, small, small, dma((1,)), dma((1,)), dma((1,)),
             dma((3, 3)), dma((3, 3)), three, three, dma((HALVES, 3, 2, 2)), dma((HALVES, 3, 2, 2)), two, two, cols, cols, cols, cols,
             out_two, out_two, out_two, out_two, out_three, out_three, out_three, out_three, out_two, out_two,
+            *[pltpu.SMEM(a.shape, jnp.int32) for a in (gate_slots, up_slots, down_slots, block_counts)],
+            dma((4,)), small,
         ],
         compiler_params=pltpu.CompilerParams(
             collective_id=0, has_side_effects=True, vmem_limit_bytes=60 * 2**20

time: 115 us -> 113 us (0.983)
  Pallas kernels: 113 us -> 111 us
    pallas_call x1, Pallas kernels: 113 us -> 111 us  [on_device(): pl.pallas_call(kernel, name='layer', out_shape=jax.ShapeDtypeStruct(token...]
where the time goes in v4:
time: 113 us; the launch traced here: 112 us
  Pallas kernels  111 us (98%)
  local copies, waits for them, and re-layouts  1.57 us (1%)
    pallas_call x1, Pallas kernels, on_device(): pl.pallas_call(kernel, name='layer', out_shape=jax.ShapeDtypeStruct(token...  111 us

profile of v4, /device:TPU:0, one launch (start us, length us, event | category | flops | bytes accessed | tf_op | source)
XLA Modules:
  0.0 112.4 jit_solution(8541701966598191257)
XLA Ops:
  0.0 110.9 %layer.1 = bf16[8,8192]{1,0:T(8,128)(2,1)} custom-call(bf16[8,8192]{1,0:T(8,128)(2,1)} %tok.1, bf16[1,84,128,128]{3,2,1,0:T(8,128)(2,1)} %gate_in.1, s32[1,84]{1,0:T(1,128)} %gate_slots_in.1, bf16[1,84,128,128]{3,2,1,0:T(8,128)(2,1)} %up_in.1, s32[1,84]{1,0:T(1,128)} %up_slots_in.1, bf16[1,84,128,128]{3,2,1,0:T(8,128)(2,1)} %down_in.1, ...), custom_call_target="tpu_custom_call" | custom-call | tf_op jit(solution)/shard_map/layer/pallas_call | solution.py:414
  110.9 1.6 %copy.10 = bf16[8,8192]{1,0:T(8,128)(2,1)} copy(bf16[8,8192]{1,0:T(8,128)(2,1)} %layer.1) | data formatting | bytes 262144

commit v5 on v4

--- a/solution.py
+++ b/solution.py
@@ -366,9 +366,9 @@
     for p in PARTS:
         start_gather4(1, p)
     project_all(0, 2, COLS)
+    swap[2].start()
     finish(0)
     end_gather4(1)
-    swap[2].start()
     project_all(1, 0, COLS)
     reorder(0)
     local[2].wait()

time: 113 us -> 113 us (level)
  no operation moved by 1% of the time
where the time goes in v5:
time: 113 us; the launch traced here: 112 us
  Pallas kernels  111 us (98%)
  local copies, waits for them, and re-layouts  1.57 us (1%)
    pallas_call x1, Pallas kernels, on_device(): pl.pallas_call(kernel, name='layer', out_shape=jax.ShapeDtypeStruct(token...  111 us

profile of v5, /device:TPU:0, one launch (start us, length us, event | category | flops | bytes accessed | tf_op | source)
XLA Modules:
  0.0 112.4 jit_solution(11881321087819326416)
XLA Ops:
  0.0 110.9 %layer.1 = bf16[8,8192]{1,0:T(8,128)(2,1)} custom-call(bf16[8,8192]{1,0:T(8,128)(2,1)} %tok.1, bf16[1,84,128,128]{3,2,1,0:T(8,128)(2,1)} %gate_in.1, s32[1,84]{1,0:T(1,128)} %gate_slots_in.1, bf16[1,84,128,128]{3,2,1,0:T(8,128)(2,1)} %up_in.1, s32[1,84]{1,0:T(1,128)} %up_slots_in.1, bf16[1,84,128,128]{3,2,1,0:T(8,128)(2,1)} %down_in.1, ...), custom_call_target="tpu_custom_call" | custom-call | tf_op jit(solution)/shard_map/layer/pallas_call | solution.py:414
  110.9 1.6 %copy.10 = bf16[8,8192]{1,0:T(8,128)(2,1)} copy(bf16[8,8192]{1,0:T(8,128)(2,1)} %layer.1) | data formatting | bytes 262144
